TPU v7x, 256 devices: a whole 4x4x8 slice. The times are simulated.
256 devices in a mesh: dp: 32 (over z_hi, x, core), seq: 8 (over y, z_lo).
Axes of the slice: x: 4, y: 4, z: 8 (z_hi: 4, z_lo: 2; z = z_hi * 2 + z_lo), core: 2. Of those that a mesh axis runs over, the one named last changes fastest.
Arguments:
- q_proj: bfloat16 [32, 1024, 4096], P('dp', 'seq'), may hold values from -200 to 200
- k_proj: bfloat16 [32, 1024, 512], P('dp', 'seq'), may hold values from -6 to 6
- v_proj: bfloat16 [32, 1024, 512], P('dp', 'seq'), may hold values from -6 to 6
- cache_k: bfloat16 [32, 1024, 512], P('dp', 'seq'), may hold values from -6 to 6
- cache_v: bfloat16 [32, 1024, 512], P('dp', 'seq'), may hold values from -6 to 6
- bias_q: bfloat16 [4096], replicated, may hold values from -3 to 3
- bias_k: bfloat16 [512], replicated, may hold values from -3 to 3
- bias_v: bfloat16 [512], replicated, may hold values from -3 to 3
- start: int32 [32], P('dp'), may hold values from 256 to 1024, as said below
- dout: bfloat16 [32, 1024, 4096], P('dp', 'seq'), may hold values from -6 to 6
Outputs:
- attn_out: bfloat16 [32, 1024, 4096], P('dp', 'seq')
- grad_q: bfloat16 [32, 1024, 4096], P('dp', 'seq')
- grad_k: bfloat16 [32, 1024, 512], P('dp', 'seq')
- grad_v: bfloat16 [32, 1024, 512], P('dp', 'seq')
- grad_bias_q: float32 [4096], replicated
- grad_bias_k: float32 [512], replicated
- grad_bias_v: float32 [512], replicated
Inputs may be any that keep to these rules, and one draw needn't show every extreme that they name: Cache slots at and beyond start hold no prefix; some sequence has a full prefix of 1024 slots.
All inputs are finite; a program needn't handle non-finite values.
Results may differ from a plain program's by a relative error of at most 0.04.
The roundings to bfloat16 on the way count: a program that leaves them out, or rounds other values in their place, can miss the bound.
Values may be sent and summed in bfloat16 or wider, within the bound.
A program may use at most 128 MiB of HBM per device.

v0:
```python
import jax
import jax.numpy as jnp
from jax import lax
from jax.sharding import PartitionSpec as P

HQ = 32
KV = 4
HD = 128
GROUP = 8


def rotary_tables(positions, width):
    half = width // 2
    freqs = jnp.exp(
        -(2.0 * jnp.arange(half, dtype=jnp.float32) / width) * jnp.log(jnp.float32(1000000.0))
    )
    angles = positions.astype(jnp.float32)[:, None] * freqs[None, :]
    cosine = jnp.concatenate([jnp.cos(angles), jnp.cos(angles)], axis=1)
    sine = jnp.concatenate([jnp.sin(angles), jnp.sin(angles)], axis=1)
    return (cosine[:, None, :], sine[:, None, :])


def rotary(values, positions):
    cosine, sine = rotary_tables(positions, values.shape[2])
    half = values.shape[2] // 2
    turned = jnp.concatenate([-values[:, :, half:], values[:, :, :half]], axis=2)
    return values * cosine + turned * sine


def rotary_back(grads, positions):
    cosine, sine = rotary_tables(positions, grads.shape[2])
    half = grads.shape[2] // 2
    scaled = grads * sine
    turned = jnp.concatenate([scaled[:, :, half:], -scaled[:, :, :half]], axis=2)
    return grads * cosine + turned


def attend(queries, cotangent, keys, values, first, row_zero, prefix):
    rows, heads, width = queries.shape
    key_count = keys.shape[0]
    slab = key_count - prefix
    head_block = max(1, min(512 // rows, GROUP, heads))
    row_block = min(rows, 512)
    scale = width ** (-0.5)
    key_index = jnp.arange(key_count, dtype=jnp.int32)

    def head_step(carry, head_slot):
        key_acc, value_acc = carry
        head_zero = head_slot * head_block
        owner = head_zero // GROUP
        key_one = lax.dynamic_index_in_dim(keys, owner, 1, keepdims=False)
        value_one = lax.dynamic_index_in_dim(values, owner, 1, keepdims=False)
        query_part = lax.dynamic_slice_in_dim(queries, head_zero, head_block, 1)
        cot_part = lax.dynamic_slice_in_dim(cotangent, head_zero, head_block, 1)

        def row_step(inner, row_slot):
            grad_key, grad_value = inner
            offset = row_slot * row_block
            query_rows = lax.dynamic_slice_in_dim(query_part, offset, row_block, 0)
            cot_rows = lax.dynamic_slice_in_dim(cot_part, offset, row_block, 0)
            query_index = row_zero + offset + jnp.arange(row_block, dtype=jnp.int32)
            allowed = jnp.where(
                key_index[None, :] < prefix,
                key_index[None, :] < first,
                key_index[None, :] - prefix <= query_index[:, None],
            )
            scores = (
                jnp.einsum("rhd,kd->hrk", query_rows, key_one, preferred_element_type=jnp.float32)
                * scale
            )
            scores = jnp.where(allowed[None], scores, -1e30)
            highest = jnp.max(scores, axis=-1, keepdims=True)
            expo = jnp.exp(scores - highest)
            probs = expo / jnp.sum(expo, axis=-1, keepdims=True)
            probs_b = probs.astype(jnp.bfloat16)
            output = jnp.einsum(
                "hrk,kd->rhd", probs_b, value_one, preferred_element_type=jnp.float32
            ).astype(jnp.bfloat16)
            delta = jnp.sum(cot_rows.astype(jnp.float32) * output.astype(jnp.float32), axis=-1).T
            dprobs = jnp.einsum(
                "rhd,kd->hrk", cot_rows, value_one, preferred_element_type=jnp.float32
            )
            dscore = (probs * (dprobs - delta[:, :, None])).astype(jnp.bfloat16)
            grad_query = (
                jnp.einsum("hrk,kd->rhd", dscore, key_one, preferred_element_type=jnp.float32)
                * scale
            ).astype(jnp.bfloat16)
            grad_key = (
                grad_key
                + jnp.einsum(
                    "hrk,rhd->kd",
                    dscore[:, :, prefix:],
                    query_rows,
                    preferred_element_type=jnp.float32,
                )
                * scale
            )
            grad_value = grad_value + jnp.einsum(
                "hrk,rhd->kd", probs_b[:, :, prefix:], cot_rows, preferred_element_type=jnp.float32
            )
            return ((grad_key, grad_value), (output, grad_query))

        empty = jnp.zeros((slab, width), jnp.float32)
        (grad_key, grad_value), (outputs, grads) = lax.scan(
            row_step, (empty, empty), jnp.arange(rows // row_block, dtype=jnp.int32)
        )
        outputs = outputs.reshape(rows, head_block, width)
        grads = grads.reshape(rows, head_block, width)
        old_key = lax.dynamic_index_in_dim(key_acc, owner, 1, keepdims=False)
        old_value = lax.dynamic_index_in_dim(value_acc, owner, 1, keepdims=False)
        key_acc = lax.dynamic_update_index_in_dim(key_acc, old_key + grad_key, owner, 1)
        value_acc = lax.dynamic_update_index_in_dim(value_acc, old_value + grad_value, owner, 1)
        return ((key_acc, value_acc), (outputs, grads))

    zeros_kv = jnp.zeros((slab, keys.shape[1], width), jnp.float32)
    (key_acc, value_acc), (outputs, grads) = lax.scan(
        head_step, (zeros_kv, zeros_kv), jnp.arange(heads // head_block, dtype=jnp.int32)
    )
    outputs = jnp.transpose(outputs, (1, 0, 2, 3)).reshape(rows, heads, width)
    grads = jnp.transpose(grads, (1, 0, 2, 3)).reshape(rows, heads, width)
    return (outputs, grads, key_acc, value_acc)


def body(q_proj, k_proj, v_proj, cache_k, cache_v, bias_q, bias_k, bias_v, start, dout):
    devices = lax.axis_size("seq")
    rank = lax.axis_index("seq")
    tokens = q_proj.shape[1]
    first = start[0]
    positions = first + rank * tokens + jnp.arange(tokens, dtype=jnp.int32)
    queries = rotary(
        (q_proj[0].astype(jnp.float32) + bias_q.astype(jnp.float32)).reshape(tokens, HQ, HD),
        positions,
    ).astype(jnp.bfloat16)
    keys = rotary(
        (k_proj[0].astype(jnp.float32) + bias_k.astype(jnp.float32)).reshape(tokens, KV, HD),
        positions,
    ).astype(jnp.bfloat16)
    values = (
        (v_proj[0].astype(jnp.float32) + bias_v.astype(jnp.float32))
        .astype(jnp.bfloat16)
        .reshape(tokens, KV, HD)
    )
    cotangent = dout[0].reshape(tokens, HQ, HD)
    cached_keys = cache_k[0].reshape(cache_k.shape[1], KV, HD)
    cached_values = cache_v[0].reshape(cache_v.shape[1], KV, HD)
    copies = max(devices // KV, 1)
    keys_wide = jnp.repeat(keys, copies, axis=1)
    values_wide = jnp.repeat(values, copies, axis=1)
    cache_keys_wide = jnp.repeat(cached_keys, copies, axis=1)
    cache_values_wide = jnp.repeat(cached_values, copies, axis=1)
    head_queries, head_keys, head_values, head_cot = (
        lax.all_to_all(queries, "seq", split_axis=1, concat_axis=0, tiled=True),
        lax.all_to_all(keys_wide, "seq", split_axis=1, concat_axis=0, tiled=True),
        lax.all_to_all(values_wide, "seq", split_axis=1, concat_axis=0, tiled=True),
        lax.all_to_all(cotangent, "seq", split_axis=1, concat_axis=0, tiled=True),
    )
    head_cache_keys, head_cache_values = (
        lax.all_to_all(cache_keys_wide, "seq", split_axis=1, concat_axis=0, tiled=True),
        lax.all_to_all(cache_values_wide, "seq", split_axis=1, concat_axis=0, tiled=True),
    )
    prefix = head_cache_keys.shape[0]
    all_keys = jnp.concatenate([head_cache_keys, head_keys], axis=0)
    all_values = jnp.concatenate([head_cache_values, head_values], axis=0)
    outputs, dq_rot, dk_rot, dv_all = attend(
        head_queries, head_cot, all_keys, all_values, first, 0, prefix
    )
    out_tokens, dq_tokens = (
        lax.all_to_all(outputs, "seq", split_axis=0, concat_axis=1, tiled=True),
        lax.all_to_all(dq_rot, "seq", split_axis=0, concat_axis=1, tiled=True),
    )
    dk_copies, dv_copies = (
        lax.all_to_all(
            dk_rot.astype(jnp.bfloat16), "seq", split_axis=0, concat_axis=1, tiled=True
        ).astype(dk_rot.dtype),
        lax.all_to_all(
            dv_all.astype(jnp.bfloat16), "seq", split_axis=0, concat_axis=1, tiled=True
        ).astype(dv_all.dtype),
    )
    dk_tokens = jnp.sum(dk_copies.reshape(tokens, KV, copies, HD), axis=2)
    dv_tokens = jnp.sum(dv_copies.reshape(tokens, KV, copies, HD), axis=2)
    grad_query = rotary_back(dq_tokens.astype(jnp.float32), positions)
    grad_key = rotary_back(dk_tokens, positions)
    sums_query, sums_key, sums_value = lax.psum(
        (
            jnp.sum(grad_query, axis=0).reshape(HQ * HD),
            jnp.sum(grad_key, axis=0).reshape(KV * HD),
            jnp.sum(dv_tokens, axis=0).reshape(KV * HD),
        ),
        ("dp", "seq"),
    )
    return (
        out_tokens.reshape(1, tokens, HQ * HD),
        grad_query.astype(jnp.bfloat16).reshape(1, tokens, HQ * HD),
        grad_key.astype(jnp.bfloat16).reshape(1, tokens, KV * HD),
        dv_tokens.astype(jnp.bfloat16).reshape(1, tokens, KV * HD),
        sums_query,
        sums_key,
        sums_value,
    )


def solution(mesh):
    placed = (
        P("dp", "seq", None),
        P("dp", "seq", None),
        P("dp", "seq", None),
        P("dp", "seq", None),
        P("dp", "seq", None),
        P(),
        P(),
        P(),
        P("dp"),
        P("dp", "seq", None),
    )
    return jax.shard_map(
        body,
        mesh=mesh,
        in_specs=placed,
        out_specs=(
            P("dp", "seq", None),
            P("dp", "seq", None),
            P("dp", "seq", None),
            P("dp", "seq", None),
            P(),
            P(),
            P(),
        ),
        check_vma=False,
    )
```

profile of v0, /device:TPU:1, one launch (start us, length us, event | category | flops | bytes accessed | tf_op | source)
XLA Modules:
  0.0 376.5 jit_solution(17324488417311112449)
XLA Ops:
  2.4 6.5 %all-to-all-start.2 = ((bf16[128,8,128]{2,0,1:T(8,128)(2,1)}), bf16[128,8,128]{2,0,1:T(8,128)(2,1)S(1)}, u32[]{:S(2)}, u32[]{:S(2)}) async-start(bf16[128,8,128]{2,0,1:T(8,128)(2,1)} %bitcast.11), calls=%async_computation.2 | async-start | bytes 524288 | tf_op jit(solution)/shard_map/all_to_all | solution.py:158
  15.8 3.4 all-to-all-start.4
  19.3 6.0 %all-to-all-done.4 = bf16[128,8,128]{2,0,1:T(8,128)(2,1)S(1)} async-done(((bf16[128,8,128]{2,0,1:T(8,128)(2,1)}), bf16[128,8,128]{2,0,1:T(8,128)(2,1)S(1)}, u32[]{:S(2)}, u32[]{:S(2)}) %all-to-all-start.4) | async-done | bytes 262176 | tf_op jit(solution)/shard_map/all_to_all | solution.py:159
  26.1 3.4 all-to-all-start.5
  29.8 5.8 %all-to-all-done.5 = bf16[128,8,128]{2,0,1:T(8,128)(2,1)S(1)} async-done(((bf16[128,8,128]{2,0,1:T(8,128)(2,1)}), bf16[128,8,128]{2,0,1:T(8,128)(2,1)S(1)}, u32[]{:S(2)}, u32[]{:S(2)}) %all-to-all-start.5) | async-done | bytes 262176 | tf_op jit(solution)/shard_map/all_to_all | solution.py:154
  36.4 3.4 all-to-all-start.3
  41.2 4.7 %all-to-all-done.3 = bf16[128,8,128]{2,0,1:T(8,128)(2,1)S(1)} async-done(((bf16[128,8,128]{2,0,1:T(8,128)(2,1)}), bf16[128,8,128]{2,0,1:T(8,128)(2,1)S(1)}, u32[]{:S(2)}, u32[]{:S(2)}) %all-to-all-start.3) | async-done | bytes 262176 | tf_op jit(solution)/shard_map/all_to_all | solution.py:153
  45.9 3.7 all-to-all-start.1
  53.5 6.5 %all-to-all-done.1 = bf16[128,32,128]{0,2,1:T(8,128)(2,1)S(1)} async-done(((bf16[128,32,128]{0,2,1:T(8,128)(2,1)}), bf16[128,32,128]{0,2,1:T(8,128)(2,1)S(1)}, u32[]{:S(2)}, u32[]{:S(2)}) %all-to-all-start.1) | async-done | bytes 1048608 | tf_op jit(solution)/shard_map/all_to_all | solution.py:155
  60.0 3.6 all-to-all-start
  66.7 7.2 %all-to-all-done = bf16[128,32,128]{2,0,1:T(8,128)(2,1)S(1)} async-done(((bf16[128,32,128]{2,0,1:T(8,128)(2,1)}), bf16[128,32,128]{2,0,1:T(8,128)(2,1)S(1)}, u32[]{:S(2)}, u32[]{:S(2)}) %all-to-all-start) | async-done | bytes 1048608 | tf_op jit(solution)/shard_map/all_to_all | solution.py:152
  75.0 139.6 %while.59 = (s32[]{:T(128)}, f32[1024,1,128]{2,0,1:T(8,128)S(1)}, f32[1024,1,128]{2,0,1:T(8,128)S(1)}, bf16[4,1024,1,128]{3,1,2,0:T(8,128)(2,1)}, bf16[4,1024,1,...) while((s32[]{:T(128)}, f32[1024,1,128]{2,0,1:T(8,128)S(1)}, ...), condition=%wide.region_6.7_spmd.clone.clone, body=%wide.region_0.6_spmd.clone.clone.sunk | while | flops 1359287296 | bytes 49224388 | solution.py:116
  79.6 28.5 %while.60 = (s32[]{:T(128)}, f32[1024,128]{1,0:T(8,128)S(1)}, f32[1024,128]{1,0:T(8,128)S(1)}, bf16[2,512,1,128]{3,1,0,2:T(8,128)(2,1)}, bf16[2,512,1,128]{3,1,2...) while((s32[]{:T(128)}, f32[1024,128]{1,0:T(8,128)S(1)}, ...), condition=%wide.region_5.5_spmd.clone.clone, body=%wide.region_1.4_spmd.clone.clone.sunk | while | flops 1359025152 | bytes 41875732 | solution.py:104
  90.1 3.1 fusion.81
  104.4 3.1 fusion.81
  114.5 28.5 %while.60 = (s32[]{:T(128)}, f32[1024,128]{1,0:T(8,128)S(1)}, f32[1024,128]{1,0:T(8,128)S(1)}, bf16[2,512,1,128]{3,1,0,2:T(8,128)(2,1)}, bf16[2,512,1,128]{3,1,2...) while((s32[]{:T(128)}, f32[1024,128]{1,0:T(8,128)S(1)}, ...), condition=%wide.region_5.5_spmd.clone.clone, body=%wide.region_1.4_spmd.clone.clone.sunk | while | flops 1359025152 | bytes 41875732 | solution.py:104
  125.0 3.1 fusion.81
  139.3 3.1 fusion.81
  149.4 28.5 %while.60 = (s32[]{:T(128)}, f32[1024,128]{1,0:T(8,128)S(1)}, f32[1024,128]{1,0:T(8,128)S(1)}, bf16[2,512,1,128]{3,1,0,2:T(8,128)(2,1)}, bf16[2,512,1,128]{3,1,2...) while((s32[]{:T(128)}, f32[1024,128]{1,0:T(8,128)S(1)}, ...), condition=%wide.region_5.5_spmd.clone.clone, body=%wide.region_1.4_spmd.clone.clone.sunk | while | flops 1359025152 | bytes 41875732 | solution.py:104
  174.2 3.1 fusion.81
  184.3 28.5 %while.60 = (s32[]{:T(128)}, f32[1024,128]{1,0:T(8,128)S(1)}, f32[1024,128]{1,0:T(8,128)S(1)}, bf16[2,512,1,128]{3,1,0,2:T(8,128)(2,1)}, bf16[2,512,1,128]{3,1,2...) while((s32[]{:T(128)}, f32[1024,128]{1,0:T(8,128)S(1)}, ...), condition=%wide.region_5.5_spmd.clone.clone, body=%wide.region_1.4_spmd.clone.clone.sunk | while | flops 1359025152 | bytes 41875732 | solution.py:104
  209.1 3.1 fusion.81
  216.8 3.4 all-to-all-start.8
  221.8 4.5 %all-to-all-done.8 = bf16[8,2,8192]{2,1,0:T(2,128)(2,1)S(1)} async-done(((bf16[8,2,8192]{2,1,0:T(2,128)(2,1)}), bf16[8,2,8192]{2,1,0:T(2,128)(2,1)S(1)}, u32[]{:S(2)}, u32[]{:S(2)}) %all-to-all-start.8) | async-done | bytes 262176 | tf_op jit(solution)/shard_map/all_to_all | solution.py:172
  226.3 3.6 all-to-all-start.9
  229.9 3.1 copy.153
  233.0 3.2 all-to-all-done.9
  236.2 3.6 all-to-all-start.6
  241.6 9.9 %all-to-all-done.6 = bf16[1024,4,128]{2,1,0:T(4,128)(2,1)S(1)} async-done(((bf16[1024,4,128]{2,1,0:T(4,128)(2,1)}), bf16[1024,4,128]{2,1,0:T(4,128)(2,1)S(1)}, u32[]{:S(2)}, u32[]{:S(2)}) %all-to-all-start.6) | async-done | bytes 1048608 | tf_op jit(solution)/shard_map/all_to_all | solution.py:168
  251.5 3.6 all-to-all-start.7
  273.0 3.2 copy.163
  286.0 90.5 %all-reduce = (f32[4096]{0:T(1024)}, f32[512]{0:T(512)}, f32[512]{0:T(512)}) all-reduce(f32[4096]{0:T(1024)S(1)} %bitcast.274, f32[512]{0:T(512)S(1)} %bitcast.276, f32[512]{0:T(512)S(1)} %bitcast.277), channel_id=1, replica_groups=mesh['dp'=32,'seq'=8] {'dp','seq'}, use_global_device_ids=true, to_apply=%region_10.11 | all-reduce | flops 5120 | bytes 40960 | tf_op jit(solution)/shard_map/psum | solution.py:183
  (322 shorter events, 159.2 us)
Async XLA Ops:
  0.6 10.7 %copy-start.22 = (bf16[1,128,512]{2,1,0:T(8,128)(2,1)S(1)}, bf16[1,128,512]{2,1,0:T(8,128)(2,1)}, u32[]{:S(2)}) copy-start(bf16[1,128,512]{2,1,0:T(8,128)(2,1)} %param.15) | copy-start | bytes 393220
  0.6 10.9 %copy-start.23 = (bf16[1,128,512]{2,1,0:T(8,128)(2,1)S(1)}, bf16[1,128,512]{2,1,0:T(8,128)(2,1)}, u32[]{:S(2)}) copy-start(bf16[1,128,512]{2,1,0:T(8,128)(2,1)} %param.18) | copy-start | bytes 393220
  2.4 16.9 %copy-start.25 = (bf16[512]{0:T(512)(128)(2,1)S(1)}, bf16[512]{0:T(512)(128)(2,1)}, u32[]{:S(2)}) copy-start(bf16[512]{0:T(512)(128)(2,1)} %param.20) | copy-start | bytes 3076
  2.4 12.7 %all-to-all-start.2 = ((bf16[128,8,128]{2,0,1:T(8,128)(2,1)}), bf16[128,8,128]{2,0,1:T(8,128)(2,1)S(1)}, u32[]{:S(2)}, u32[]{:S(2)}) async-start(bf16[128,8,128]{2,0,1:T(8,128)(2,1)} %bitcast.11), calls=%async_computation.2 | async-start | bytes 524288 | tf_op jit(solution)/shard_map/all_to_all | solution.py:158
  12.1 37.5 %copy-start.8 = (f32[128,128]{1,0:T(8,128)}, f32[128,128]{1,0:T(8,128)S(1)}, u32[]{:S(2)}) copy-start(f32[128,128]{1,0:T(8,128)S(1)} %get-tuple-element.735) | copy-start | bytes 196612
  12.1 37.6 %copy-start.6 = (f32[128,128]{1,0:T(8,128)}, f32[128,128]{1,0:T(8,128)S(1)}, u32[]{:S(2)}) copy-start(f32[128,128]{1,0:T(8,128)S(1)} %get-tuple-element.734) | copy-start | bytes 196612
  15.8 9.5 %all-to-all-start.4 = ((bf16[128,8,128]{2,0,1:T(8,128)(2,1)}), bf16[128,8,128]{2,0,1:T(8,128)(2,1)S(1)}, u32[]{:S(2)}, u32[]{:S(2)}) async-start(bf16[128,8,128]{2,0,1:T(8,128)(2,1)} %bitcast.21), calls=%async_computation.4 | async-start | bytes 524288 | tf_op jit(solution)/shard_map/all_to_all | solution.py:159
  19.3 20.5 %copy-start.10 = (bf16[1,128,4096]{2,1,0:T(8,128)(2,1)S(1)}, bf16[1,128,4096]{2,1,0:T(8,128)(2,1)}, u32[]{:S(2)}) copy-start(bf16[1,128,4096]{2,1,0:T(8,128)(2,1)} %param.23) | copy-start | bytes 3145732
  25.3 15.8 %copy-start.13 = (bf16[128,8,128]{2,0,1:T(8,128)(2,1)}, bf16[128,8,128]{2,0,1:T(8,128)(2,1)S(1)}, u32[]{:S(2)}) copy-start(bf16[128,8,128]{2,0,1:T(8,128)(2,1)S(1)} %all-to-all-done.4) | copy-start | bytes 786436
  26.1 9.5 %all-to-all-start.5 = ((bf16[128,8,128]{2,0,1:T(8,128)(2,1)}), bf16[128,8,128]{2,0,1:T(8,128)(2,1)S(1)}, u32[]{:S(2)}, u32[]{:S(2)}) async-start(bf16[128,8,128]{2,0,1:T(8,128)(2,1)} %bitcast.26), calls=%async_computation.5 | async-start | bytes 524288 | tf_op jit(solution)/shard_map/all_to_all | solution.py:154
  36.4 9.5 %all-to-all-start.3 = ((bf16[128,8,128]{2,0,1:T(8,128)(2,1)}), bf16[128,8,128]{2,0,1:T(8,128)(2,1)S(1)}, u32[]{:S(2)}, u32[]{:S(2)}) async-start(bf16[128,8,128]{2,0,1:T(8,128)(2,1)} %bitcast.17), calls=%async_computation.3 | async-start | bytes 524288 | tf_op jit(solution)/shard_map/all_to_all | solution.py:153
  39.8 10.0 %copy-start.11 = (bf16[1,128,4096]{2,1,0:T(8,128)(2,1)S(1)}, bf16[1,128,4096]{2,1,0:T(8,128)(2,1)}, u32[]{:S(2)}) copy-start(bf16[1,128,4096]{2,1,0:T(8,128)(2,1)} %param.14) | copy-start | bytes 3145732
  45.9 3.8 %copy-start.17 = (bf16[128,8,128]{2,0,1:T(8,128)(2,1)}, bf16[128,8,128]{2,0,1:T(8,128)(2,1)S(1)}, u32[]{:S(2)}) copy-start(bf16[128,8,128]{2,0,1:T(8,128)(2,1)S(1)} %all-to-all-done.3) | copy-start | bytes 786436
  45.9 4.6 %copy-start.24 = (bf16[4096]{0:T(1024)(128)(2,1)S(1)}, bf16[4096]{0:T(1024)(128)(2,1)}, u32[]{:S(2)}) copy-start(bf16[4096]{0:T(1024)(128)(2,1)} %param.19) | copy-start | bytes 24580
  45.9 14.1 %all-to-all-start.1 = ((bf16[128,32,128]{0,2,1:T(8,128)(2,1)}), bf16[128,32,128]{0,2,1:T(8,128)(2,1)S(1)}, u32[]{:S(2)}, u32[]{:S(2)}) async-start(bf16[128,32,128]{0,2,1:T(8,128)(2,1)} %bitcast.6), calls=%async_computation.1 | async-start | bytes 2097152 | tf_op jit(solution)/shard_map/all_to_all | solution.py:155
  52.2 11.4 %copy-start.14 = (bf16[128,8,128]{2,0,1:T(8,128)(2,1)S(1)}, bf16[128,8,128]{2,0,1:T(8,128)(2,1)}, u32[]{:S(2)}) copy-start(bf16[128,8,128]{2,0,1:T(8,128)(2,1)} %copy-done.13) | copy-start | bytes 786436
  52.2 11.4 %copy-start.16 = (bf16[128,8,128]{2,0,1:T(8,128)(2,1)S(1)}, bf16[128,8,128]{2,0,1:T(8,128)(2,1)}, u32[]{:S(2)}) copy-start(bf16[128,8,128]{2,0,1:T(8,128)(2,1)} %copy-done.15) | copy-start | bytes 786436
  60.0 13.9 %all-to-all-start = ((bf16[128,32,128]{2,0,1:T(8,128)(2,1)}), bf16[128,32,128]{2,0,1:T(8,128)(2,1)S(1)}, u32[]{:S(2)}, u32[]{:S(2)}) async-start(bf16[128,32,128]{2,0,1:T(8,128)(2,1)} %copy.142), calls=%async_computation | async-start | bytes 2097152 | tf_op jit(solution)/shard_map/all_to_all | solution.py:152
  89.4 3.7 copy-start
  103.7 3.8 copy-start
  124.3 3.7 copy-start
  138.6 3.8 copy-start
  159.3 3.7 copy-start
  173.5 3.8 copy-start
  194.2 3.7 copy-start
  208.4 3.8 copy-start
  216.8 9.5 %all-to-all-start.8 = ((bf16[8,2,8192]{2,1,0:T(2,128)(2,1)}), bf16[8,2,8192]{2,1,0:T(2,128)(2,1)S(1)}, u32[]{:S(2)}, u32[]{:S(2)}) async-start(bf16[8,2,8192]{2,1,0:T(2,128)(2,1)} %reshape.436), calls=%async_computation.8 | async-start | bytes 524288 | tf_op jit(solution)/shard_map/all_to_all | solution.py:172
  226.3 10.0 %all-to-all-start.9 = ((bf16[8,2,8192]{2,1,0:T(2,128)(2,1)}), bf16[8,2,8192]{2,1,0:T(2,128)(2,1)S(1)}, u32[]{:S(2)}, u32[]{:S(2)}) async-start(bf16[8,2,8192]{2,1,0:T(2,128)(2,1)} %reshape.438), calls=%async_computation.9 | async-start | bytes 524288 | tf_op jit(solution)/shard_map/all_to_all | solution.py:175
  229.9 9.9 %copy-start.12 = (bf16[4,1024,1,128]{3,1,2,0:T(8,128)(2,1)S(1)}, bf16[4,1024,1,128]{3,1,2,0:T(8,128)(2,1)}, u32[]{:S(2)}) copy-start(bf16[4,1024,1,128]{3,1,2,0:T(8,128)(2,1)} %get-tuple-element.348) | copy-start | bytes 3145732
  236.2 15.3 %all-to-all-start.6 = ((bf16[1024,4,128]{2,1,0:T(4,128)(2,1)}), bf16[1024,4,128]{2,1,0:T(4,128)(2,1)S(1)}, u32[]{:S(2)}, u32[]{:S(2)}) async-start(bf16[1024,4,128]{2,1,0:T(4,128)(2,1)} %copy.153), calls=%async_computation.6 | async-start | bytes 2097152 | tf_op jit(solution)/shard_map/all_to_all | solution.py:168
  251.5 16.6 %all-to-all-start.7 = ((bf16[1024,4,128]{2,1,0:T(4,128)(2,1)}), bf16[1024,4,128]{2,1,0:T(4,128)(2,1)S(1)}, u32[]{:S(2)}, u32[]{:S(2)}) async-start(bf16[1024,4,128]{2,1,0:T(4,128)(2,1)} %bitcast.260), calls=%async_computation.7 | async-start | bytes 2097152 | tf_op jit(solution)/shard_map/all_to_all | solution.py:169
  255.4 5.0 %copy-start.9 = (f32[128,128]{1,0:T(8,128)S(1)}, f32[128,128]{1,0:T(8,128)}, u32[]{:S(2)}) copy-start(f32[128,128]{1,0:T(8,128)} %copy-done.8) | copy-start | bytes 196612
  (17 other events, 30.5 us)
where the time goes:
time: 379 us; the launch traced here: 376 us
  blocking collectives  90.5 us (24%)
  matrix products  79 us (21%)
  local copies, waits for them, and re-layouts  62 us (16%)
  waiting for transfers between devices  53.1 us (14%)
  starting transfers between devices  38.1 us (10%)
  other arithmetic  37.6 us (10%)
  loops' own time  14.1 us (4%)
    psum x1, blocking collectives, body(): lax.psum((jnp.sum(grad_query, axis=0).reshape(HQ * HD), jnp.sum(grad_key,...  90.5 us
    dot_general x8, matrix products, row_step(): jnp.einsum('hrk,kd->rhd', dscore, key_one, preferred_element_type=jnp.flo...  24.6 us
    dot_general x8, matrix products, row_step(): jnp.einsum('rhd,kd->hrk', cot_rows, value_one, preferred_element_type=jnp...  19.4 us
    dot_general x8, matrix products, row_step(): jnp.einsum('rhd,kd->hrk', query_rows, key_one, preferred_element_type=jnp...  18.6 us
    all_to_all x1, waiting for transfers between devices, body(): lax.all_to_all(outputs, 'seq', split_axis=0, concat_axis=1, tiled=True)  9.94 us
    another operation x1, loops' own time, attend(): lax.scan(head_step, (zeros_kv, zeros_kv), jnp.arange(heads // head_block,...  8.13 us
    unnamed x57, local copies, waits for them, and re-layouts  7.6 us
  transfers between devices with their start and end apart: 10, of which 10 were waited for; matrix products, arithmetic and copies ran while one was open for 7% of the time, Pallas kernels for 0%

commit v1 on v0

--- a/solution.py
+++ b/solution.py
@@ -152,7 +152,12 @@
         lax.all_to_all(queries, "seq", split_axis=1, concat_axis=0, tiled=True),
         lax.all_to_all(keys_wide, "seq", split_axis=1, concat_axis=0, tiled=True),
         lax.all_to_all(values_wide, "seq", split_axis=1, concat_axis=0, tiled=True),
-        lax.all_to_all(cotangent, "seq", split_axis=1, concat_axis=0, tiled=True),
+        jnp.concatenate(
+            lax.all_to_all(
+                jnp.stack(jnp.split(cotangent, lax.axis_size("seq"), axis=1)), "seq", 0, 0
+            ),
+            axis=0,
+        ),
     )
     head_cache_keys, head_cache_values = (
         lax.all_to_all(cache_keys_wide, "seq", split_axis=1, concat_axis=0, tiled=True),

time: 379 us -> 390 us (1.029)
  local copies, waits for them, and re-layouts: 62 us -> 73 us
  waiting for transfers between devices: 53.1 us -> 48.7 us
    split x0 -> x9, local copies, waits for them, and re-layouts: none -> 7.15 us  [body(): jnp.split(cotangent, lax.axis_size('seq'), axis=1)]
    unnamed x57 -> x76, local copies, waits for them, and re-layouts: 7.6 us -> 8.68 us
  transfers between devices with their start and end apart: 10 -> 10, of which waited for: 10 -> 9; matrix products, arithmetic and copies ran while one was open for 7% -> 10% of each run, Pallas kernels for 0% -> 0%
where the time goes in v1:
time: 390 us; the launch traced here: 388 us
  blocking collectives  90.7 us (23%)
  matrix products  79.2 us (20%)
  local copies, waits for them, and re-layouts  73 us (19%)
  waiting for transfers between devices  48.7 us (12%)
  starting transfers between devices  41.3 us (11%)
  other arithmetic  38.4 us (10%)
  loops' own time  14.2 us (4%)
    psum x1, blocking collectives, body(): lax.psum((jnp.sum(grad_query, axis=0).reshape(HQ * HD), jnp.sum(grad_key,...  90.7 us
    dot_general x8, matrix products, row_step(): jnp.einsum('hrk,kd->rhd', dscore, key_one, preferred_element_type=jnp.flo...  24.7 us
    dot_general x8, matrix products, row_step(): jnp.einsum('rhd,kd->hrk', cot_rows, value_one, preferred_element_type=jnp...  19.5 us
    dot_general x8, matrix products, row_step(): jnp.einsum('rhd,kd->hrk', query_rows, key_one, preferred_element_type=jnp...  18.5 us
    all_to_all x1, waiting for transfers between devices, body(): lax.all_to_all(queries, 'seq', split_axis=1, concat_axis=0, tiled=True)  9.26 us
    all_to_all x1, waiting for transfers between devices, body(): lax.all_to_all(outputs, 'seq', split_axis=0, concat_axis=1, tiled=True)  9.24 us
    unnamed x76, local copies, waits for them, and re-layouts  8.68 us
    another operation x1, loops' own time, attend(): lax.scan(head_step, (zeros_kv, zeros_kv), jnp.arange(heads // head_block,...  8.2 us
  transfers between devices with their start and end apart: 10, of which 9 were waited for; matrix products, arithmetic and copies ran while one was open for 10% of the time, Pallas kernels for 0%

profile of v1, /device:TPU:1, one launch (start us, length us, event | category | flops | bytes accessed | tf_op | source)
XLA Modules:
  0.0 387.5 jit_solution(6441683339130237077)
XLA Ops:
  2.4 6.4 %all-to-all-start.2 = ((bf16[128,8,128]{2,0,1:T(8,128)(2,1)}), bf16[128,8,128]{2,0,1:T(8,128)(2,1)}, u32[]{:S(2)}, u32[]{:S(2)}) async-start(bf16[128,8,128]{2,0,1:T(8,128)(2,1)} %bitcast.16), calls=%async_computation.2 | async-start | bytes 524288 | tf_op jit(solution)/shard_map/all_to_all | solution.py:163
  23.2 5.1 %all-to-all-start.4 = ((bf16[128,8,128]{2,0,1:T(8,128)(2,1)}), bf16[128,8,128]{2,0,1:T(8,128)(2,1)S(1)}, u32[]{:S(2)}, u32[]{:S(2)}) async-start(bf16[128,8,128]{2,0,1:T(8,128)(2,1)} %bitcast.26), calls=%async_computation.4 | async-start | bytes 524288 | tf_op jit(solution)/shard_map/all_to_all | solution.py:164
  29.3 5.2 %all-to-all-done.4 = bf16[128,8,128]{2,0,1:T(8,128)(2,1)S(1)} async-done(((bf16[128,8,128]{2,0,1:T(8,128)(2,1)}), bf16[128,8,128]{2,0,1:T(8,128)(2,1)S(1)}, u32[]{:S(2)}, u32[]{:S(2)}) %all-to-all-start.4) | async-done | bytes 262176 | tf_op jit(solution)/shard_map/all_to_all | solution.py:164
  35.3 4.1 %all-to-all-start.5 = ((bf16[128,8,128]{2,0,1:T(8,128)(2,1)}), bf16[128,8,128]{2,0,1:T(8,128)(2,1)}, u32[]{:S(2)}, u32[]{:S(2)}) async-start(bf16[128,8,128]{2,0,1:T(8,128)(2,1)} %bitcast.31), calls=%async_computation.5 | async-start | bytes 524288 | tf_op jit(solution)/shard_map/all_to_all | solution.py:154
  40.0 5.5 %all-to-all-done.5 = bf16[128,8,128]{2,0,1:T(8,128)(2,1)} async-done(((bf16[128,8,128]{2,0,1:T(8,128)(2,1)}), bf16[128,8,128]{2,0,1:T(8,128)(2,1)}, u32[]{:S(2)}, u32[]{:S(2)}) %all-to-all-start.5) | async-done | bytes 262176 | tf_op jit(solution)/shard_map/all_to_all | solution.py:154
  47.1 4.0 %all-to-all-start.3 = ((bf16[128,8,128]{2,0,1:T(8,128)(2,1)}), bf16[128,8,128]{2,0,1:T(8,128)(2,1)}, u32[]{:S(2)}, u32[]{:S(2)}) async-start(bf16[128,8,128]{2,0,1:T(8,128)(2,1)} %bitcast.22), calls=%async_computation.3 | async-start | bytes 524288 | tf_op jit(solution)/shard_map/all_to_all | solution.py:153
  54.2 3.2 all-to-all-done.3
  57.3 3.6 all-to-all-start
  62.2 9.3 %all-to-all-done = bf16[128,32,128]{2,0,1:T(8,128)(2,1)S(1)} async-done(((bf16[128,32,128]{2,0,1:T(8,128)(2,1)}), bf16[128,32,128]{2,0,1:T(8,128)(2,1)S(1)}, u32[]{:S(2)}, u32[]{:S(2)}) %all-to-all-start) | async-done | bytes 1048608 | tf_op jit(solution)/shard_map/all_to_all | solution.py:152
  71.4 4.0 %all-to-all-start.1 = ((bf16[8,128,4,128]{3,1,2,0:T(8,128)(2,1)}), bf16[8,128,4,128]{3,1,2,0:T(8,128)(2,1)S(1)}, u32[]{:S(2)}, u32[]{:S(2)}) async-start(bf16[8,128,4,128]{3,1,2,0:T(8,128)(2,1)} %copy-done.8), calls=%async_computation.1 | async-start | bytes 2097152 | tf_op jit(solution)/shard_map/all_to_all | solution.py:156
  78.5 7.2 %all-to-all-done.1 = bf16[8,128,4,128]{3,1,2,0:T(8,128)(2,1)S(1)} async-done(((bf16[8,128,4,128]{3,1,2,0:T(8,128)(2,1)}), bf16[8,128,4,128]{3,1,2,0:T(8,128)(2,1)S(1)}, u32[]{:S(2)}, u32[]{:S(2)}) %all-to-all-start.1) | async-done | bytes 1048608 | tf_op jit(solution)/shard_map/all_to_all | solution.py:156
  86.9 140.3 %while.59 = (s32[]{:T(128)}, f32[1024,1,128]{2,0,1:T(8,128)S(1)}, f32[1024,1,128]{2,0,1:T(8,128)S(1)}, bf16[4,1024,1,128]{3,1,2,0:T(8,128)(2,1)}, bf16[4,1024,1,...) while((s32[]{:T(128)}, f32[1024,1,128]{2,0,1:T(8,128)S(1)}, ...), condition=%wide.region_6.7_spmd.clone.clone, body=%wide.region_0.6_spmd.clone.clone.sunk | while | flops 1359287296 | bytes 53418744 | solution.py:116
  91.6 28.6 %while.60 = (s32[]{:T(128)}, f32[1024,128]{1,0:T(8,128)S(1)}, f32[1024,128]{1,0:T(8,128)S(1)}, bf16[2,512,1,128]{3,1,0,2:T(8,128)(2,1)}, bf16[2,512,1,128]{3,1,2...) while((s32[]{:T(128)}, f32[1024,128]{1,0:T(8,128)S(1)}, ...), condition=%wide.region_5.5_spmd.clone.clone, body=%wide.region_1.4_spmd.clone.clone.sunk | while | flops 1359025152 | bytes 41875732 | solution.py:104
  102.1 3.1 fusion.82
  116.4 3.1 fusion.82
  126.6 28.6 %while.60 = (s32[]{:T(128)}, f32[1024,128]{1,0:T(8,128)S(1)}, f32[1024,128]{1,0:T(8,128)S(1)}, bf16[2,512,1,128]{3,1,0,2:T(8,128)(2,1)}, bf16[2,512,1,128]{3,1,2...) while((s32[]{:T(128)}, f32[1024,128]{1,0:T(8,128)S(1)}, ...), condition=%wide.region_5.5_spmd.clone.clone, body=%wide.region_1.4_spmd.clone.clone.sunk | while | flops 1359025152 | bytes 41875732 | solution.py:104
  137.2 3.1 fusion.82
  161.7 28.6 %while.60 = (s32[]{:T(128)}, f32[1024,128]{1,0:T(8,128)S(1)}, f32[1024,128]{1,0:T(8,128)S(1)}, bf16[2,512,1,128]{3,1,0,2:T(8,128)(2,1)}, bf16[2,512,1,128]{3,1,2...) while((s32[]{:T(128)}, f32[1024,128]{1,0:T(8,128)S(1)}, ...), condition=%wide.region_5.5_spmd.clone.clone, body=%wide.region_1.4_spmd.clone.clone.sunk | while | flops 1359025152 | bytes 41875732 | solution.py:104
  172.3 3.1 fusion.82
  186.6 3.1 fusion.82
  196.8 28.6 %while.60 = (s32[]{:T(128)}, f32[1024,128]{1,0:T(8,128)S(1)}, f32[1024,128]{1,0:T(8,128)S(1)}, bf16[2,512,1,128]{3,1,0,2:T(8,128)(2,1)}, bf16[2,512,1,128]{3,1,2...) while((s32[]{:T(128)}, f32[1024,128]{1,0:T(8,128)S(1)}, ...), condition=%wide.region_5.5_spmd.clone.clone, body=%wide.region_1.4_spmd.clone.clone.sunk | while | flops 1359025152 | bytes 41875732 | solution.py:104
  207.4 3.1 fusion.82
  221.7 3.1 fusion.82
  229.4 3.4 all-to-all-start.8
  234.4 4.5 %all-to-all-done.8 = bf16[8,2,8192]{2,1,0:T(2,128)(2,1)S(1)} async-done(((bf16[8,2,8192]{2,1,0:T(2,128)(2,1)}), bf16[8,2,8192]{2,1,0:T(2,128)(2,1)S(1)}, u32[]{:S(2)}, u32[]{:S(2)}) %all-to-all-start.8) | async-done | bytes 262176 | tf_op jit(solution)/shard_map/all_to_all | solution.py:177
  238.8 3.4 all-to-all-start.9
  242.3 3.1 copy.196
  248.3 3.6 all-to-all-start.6
  253.7 9.2 %all-to-all-done.6 = bf16[1024,4,128]{2,1,0:T(4,128)(2,1)S(1)} async-done(((bf16[1024,4,128]{2,1,0:T(4,128)(2,1)}), bf16[1024,4,128]{2,1,0:T(4,128)(2,1)S(1)}, u32[]{:S(2)}, u32[]{:S(2)}) %all-to-all-start.6) | async-done | bytes 1048608 | tf_op jit(solution)/shard_map/all_to_all | solution.py:173
  262.9 3.8 all-to-all-start.7
  283.9 3.2 copy.206
  296.9 90.7 %all-reduce = (f32[4096]{0:T(1024)}, f32[512]{0:T(512)}, f32[512]{0:T(512)}) all-reduce(f32[4096]{0:T(1024)S(1)} %bitcast.286, f32[512]{0:T(512)S(1)} %bitcast.288, f32[512]{0:T(512)S(1)} %bitcast.289), channel_id=1, replica_groups=mesh['dp'=32,'seq'=8] {'dp','seq'}, use_global_device_ids=true, to_apply=%region_10.11 | all-reduce | flops 5120 | bytes 40960 | tf_op jit(solution)/shard_map/psum | solution.py:188
  (367 shorter events, 167.4 us)
Async XLA Ops:
  0.6 11.4 %copy-start.30 = (bf16[1,128,512]{2,1,0:T(8,128)(2,1)S(1)}, bf16[1,128,512]{2,1,0:T(8,128)(2,1)}, u32[]{:S(2)}) copy-start(bf16[1,128,512]{2,1,0:T(8,128)(2,1)} %param.15) | copy-start | bytes 393220
  0.6 11.7 %copy-start.31 = (bf16[1,128,512]{2,1,0:T(8,128)(2,1)S(1)}, bf16[1,128,512]{2,1,0:T(8,128)(2,1)}, u32[]{:S(2)}) copy-start(bf16[1,128,512]{2,1,0:T(8,128)(2,1)} %param.18) | copy-start | bytes 393220
  0.7 12.4 %copy-start.29 = (bf16[1,128,512]{2,1,0:T(8,128)(2,1)S(1)}, bf16[1,128,512]{2,1,0:T(8,128)(2,1)}, u32[]{:S(2)}) copy-start(bf16[1,128,512]{2,1,0:T(8,128)(2,1)} %param.16) | copy-start | bytes 393220
  1.7 12.2 %copy-start.11 = (bf16[1,128,4096]{2,1,0:T(8,128)(2,1)S(1)}, bf16[1,128,4096]{2,1,0:T(8,128)(2,1)}, u32[]{:S(2)}) copy-start(bf16[1,128,4096]{2,1,0:T(8,128)(2,1)} %param.14) | copy-start | bytes 3145732
  2.4 20.0 %all-to-all-start.2 = ((bf16[128,8,128]{2,0,1:T(8,128)(2,1)}), bf16[128,8,128]{2,0,1:T(8,128)(2,1)}, u32[]{:S(2)}, u32[]{:S(2)}) async-start(bf16[128,8,128]{2,0,1:T(8,128)(2,1)} %bitcast.16), calls=%async_computation.2 | async-start | bytes 524288 | tf_op jit(solution)/shard_map/all_to_all | solution.py:163
  10.6 17.9 %copy-start.6 = (f32[128,128]{1,0:T(8,128)}, f32[128,128]{1,0:T(8,128)S(1)}, u32[]{:S(2)}) copy-start(f32[128,128]{1,0:T(8,128)S(1)} %get-tuple-element.742) | copy-start | bytes 196612
  10.6 17.9 %copy-start.9 = (f32[128,128]{1,0:T(8,128)}, f32[128,128]{1,0:T(8,128)S(1)}, u32[]{:S(2)}) copy-start(f32[128,128]{1,0:T(8,128)S(1)} %get-tuple-element.743) | copy-start | bytes 196612
  15.2 7.2 %copy-start.33 = (bf16[512]{0:T(512)(128)(2,1)S(1)}, bf16[512]{0:T(512)(128)(2,1)}, u32[]{:S(2)}) copy-start(bf16[512]{0:T(512)(128)(2,1)} %param.20) | copy-start | bytes 3076
  15.2 7.2 %copy-start.19 = (bf16[128,4,128]{2,0,1:T(8,128)(2,1)S(1)}, bf16[128,4,128]{2,0,1:T(8,128)(2,1)}, u32[]{:S(2)}) copy-start(bf16[128,4,128]{2,0,1:T(8,128)(2,1)} %copy.193) | copy-start | bytes 393220
  20.9 13.7 %copy-start.18 = (bf16[128,4,128]{2,0,1:T(8,128)(2,1)S(1)}, bf16[128,4,128]{2,0,1:T(8,128)(2,1)}, u32[]{:S(2)}) copy-start(bf16[128,4,128]{2,0,1:T(8,128)(2,1)} %copy.194) | copy-start | bytes 393220
  22.4 16.9 %copy-start.32 = (bf16[4096]{0:T(1024)(128)(2,1)S(1)}, bf16[4096]{0:T(1024)(128)(2,1)}, u32[]{:S(2)}) copy-start(bf16[4096]{0:T(1024)(128)(2,1)} %param.19) | copy-start | bytes 24580
  23.2 11.3 %all-to-all-start.4 = ((bf16[128,8,128]{2,0,1:T(8,128)(2,1)}), bf16[128,8,128]{2,0,1:T(8,128)(2,1)S(1)}, u32[]{:S(2)}, u32[]{:S(2)}) async-start(bf16[128,8,128]{2,0,1:T(8,128)(2,1)} %bitcast.26), calls=%async_computation.4 | async-start | bytes 524288 | tf_op jit(solution)/shard_map/all_to_all | solution.py:164
  35.3 10.2 %all-to-all-start.5 = ((bf16[128,8,128]{2,0,1:T(8,128)(2,1)}), bf16[128,8,128]{2,0,1:T(8,128)(2,1)}, u32[]{:S(2)}, u32[]{:S(2)}) async-start(bf16[128,8,128]{2,0,1:T(8,128)(2,1)} %bitcast.31), calls=%async_computation.5 | async-start | bytes 524288 | tf_op jit(solution)/shard_map/all_to_all | solution.py:154
  47.1 10.2 %all-to-all-start.3 = ((bf16[128,8,128]{2,0,1:T(8,128)(2,1)}), bf16[128,8,128]{2,0,1:T(8,128)(2,1)}, u32[]{:S(2)}, u32[]{:S(2)}) async-start(bf16[128,8,128]{2,0,1:T(8,128)(2,1)} %bitcast.22), calls=%async_computation.3 | async-start | bytes 524288 | tf_op jit(solution)/shard_map/all_to_all | solution.py:153
  52.8 8.1 %copy-start.28 = (bf16[128,4,128]{2,0,1:T(8,128)(2,1)S(1)}, bf16[128,4,128]{2,0,1:T(8,128)(2,1)}, u32[]{:S(2)}) copy-start(bf16[128,4,128]{2,0,1:T(8,128)(2,1)} %copy.181) | copy-start | bytes 393220
  52.8 8.1 %copy-start.27 = (bf16[128,4,128]{2,0,1:T(8,128)(2,1)S(1)}, bf16[128,4,128]{2,0,1:T(8,128)(2,1)}, u32[]{:S(2)}) copy-start(bf16[128,4,128]{2,0,1:T(8,128)(2,1)} %copy.182) | copy-start | bytes 393220
  52.8 8.1 %copy-start.26 = (bf16[128,4,128]{2,0,1:T(8,128)(2,1)S(1)}, bf16[128,4,128]{2,0,1:T(8,128)(2,1)}, u32[]{:S(2)}) copy-start(bf16[128,4,128]{2,0,1:T(8,128)(2,1)} %copy.183) | copy-start | bytes 393220
  52.8 8.2 %copy-start.25 = (bf16[128,4,128]{2,0,1:T(8,128)(2,1)S(1)}, bf16[128,4,128]{2,0,1:T(8,128)(2,1)}, u32[]{:S(2)}) copy-start(bf16[128,4,128]{2,0,1:T(8,128)(2,1)} %copy.184) | copy-start | bytes 393220
  54.1 6.9 %copy-start.24 = (bf16[128,4,128]{2,0,1:T(8,128)(2,1)S(1)}, bf16[128,4,128]{2,0,1:T(8,128)(2,1)}, u32[]{:S(2)}) copy-start(bf16[128,4,128]{2,0,1:T(8,128)(2,1)} %copy.185) | copy-start | bytes 393220
  54.2 6.9 %copy-start.23 = (bf16[128,4,128]{2,0,1:T(8,128)(2,1)S(1)}, bf16[128,4,128]{2,0,1:T(8,128)(2,1)}, u32[]{:S(2)}) copy-start(bf16[128,4,128]{2,0,1:T(8,128)(2,1)} %copy.187) | copy-start | bytes 393220
  54.2 7.0 %copy-start.22 = (bf16[128,4,128]{2,0,1:T(8,128)(2,1)S(1)}, bf16[128,4,128]{2,0,1:T(8,128)(2,1)}, u32[]{:S(2)}) copy-start(bf16[128,4,128]{2,0,1:T(8,128)(2,1)} %copy.188) | copy-start | bytes 393220
  57.3 14.1 %all-to-all-start = ((bf16[128,32,128]{2,0,1:T(8,128)(2,1)}), bf16[128,32,128]{2,0,1:T(8,128)(2,1)S(1)}, u32[]{:S(2)}, u32[]{:S(2)}) async-start(bf16[128,32,128]{2,0,1:T(8,128)(2,1)} %copy.178), calls=%async_computation | async-start | bytes 2097152 | tf_op jit(solution)/shard_map/all_to_all | solution.py:152
  71.4 14.3 %all-to-all-start.1 = ((bf16[8,128,4,128]{3,1,2,0:T(8,128)(2,1)}), bf16[8,128,4,128]{3,1,2,0:T(8,128)(2,1)S(1)}, u32[]{:S(2)}, u32[]{:S(2)}) async-start(bf16[8,128,4,128]{3,1,2,0:T(8,128)(2,1)} %copy-done.8), calls=%async_computation.1 | async-start | bytes 2097152 | tf_op jit(solution)/shard_map/all_to_all | solution.py:156
  101.5 3.8 copy-start
  136.5 3.8 copy-start
  206.7 3.8 copy-start
  229.4 9.5 %all-to-all-start.8 = ((bf16[8,2,8192]{2,1,0:T(2,128)(2,1)}), bf16[8,2,8192]{2,1,0:T(2,128)(2,1)S(1)}, u32[]{:S(2)}, u32[]{:S(2)}) async-start(bf16[8,2,8192]{2,1,0:T(2,128)(2,1)} %reshape.440), calls=%async_computation.8 | async-start | bytes 524288 | tf_op jit(solution)/shard_map/all_to_all | solution.py:177
  238.8 9.5 %all-to-all-start.9 = ((bf16[8,2,8192]{2,1,0:T(2,128)(2,1)}), bf16[8,2,8192]{2,1,0:T(2,128)(2,1)S(1)}, u32[]{:S(2)}, u32[]{:S(2)}) async-start(bf16[8,2,8192]{2,1,0:T(2,128)(2,1)} %reshape.442), calls=%async_computation.9 | async-start | bytes 524288 | tf_op jit(solution)/shard_map/all_to_all | solution.py:180
  242.3 9.6 %copy-start.13 = (bf16[4,1024,1,128]{3,1,2,0:T(8,128)(2,1)S(1)}, bf16[4,1024,1,128]{3,1,2,0:T(8,128)(2,1)}, u32[]{:S(2)}) copy-start(bf16[4,1024,1,128]{3,1,2,0:T(8,128)(2,1)} %get-tuple-element.348) | copy-start | bytes 3145732
  248.3 14.6 %all-to-all-start.6 = ((bf16[1024,4,128]{2,1,0:T(4,128)(2,1)}), bf16[1024,4,128]{2,1,0:T(4,128)(2,1)S(1)}, u32[]{:S(2)}, u32[]{:S(2)}) async-start(bf16[1024,4,128]{2,1,0:T(4,128)(2,1)} %copy.196), calls=%async_computation.6 | async-start | bytes 2097152 | tf_op jit(solution)/shard_map/all_to_all | solution.py:173
  262.9 16.0 %all-to-all-start.7 = ((bf16[1024,4,128]{2,1,0:T(4,128)(2,1)}), bf16[1024,4,128]{2,1,0:T(4,128)(2,1)S(1)}, u32[]{:S(2)}, u32[]{:S(2)}) async-start(bf16[1024,4,128]{2,1,0:T(4,128)(2,1)} %bitcast.273), calls=%async_computation.7 | async-start | bytes 2097152 | tf_op jit(solution)/shard_map/all_to_all | solution.py:174
  267.1 5.0 %copy-start.10 = (f32[128,128]{1,0:T(8,128)S(1)}, f32[128,128]{1,0:T(8,128)}, u32[]{:S(2)}) copy-start(f32[128,128]{1,0:T(8,128)} %copy-done.9) | copy-start | bytes 196612
  (31 other events, 68.1 us)
